TPU v7x, 32 devices: a whole 2x2x4 slice. The times are simulated.
32 devices in a mesh: section: 2 (over core), dp: 8 (over z, x), rep: 2 (over y).
Axes of the slice: x: 2, y: 2, z: 4, core: 2. Of those that a mesh axis runs over, the one named last changes fastest.
Arguments:
- inputs: bfloat16 [4096, 1024], P(('dp', 'rep')), may hold values from -6 to 6
- cotangent: bfloat16 [4096, 1024], P(('dp', 'rep')), may hold values from -6 to 6
- seg_counts: int32 [256], P(('dp', 'rep')), may hold values from 2 to 16
- w_qkv: bfloat16 [2, 1024, 3072], P('section'), may hold values from -0.1875 to 0.1875
- w_out: bfloat16 [2, 1024, 1024], P('section'), may hold values from -0.375 to 0.375
- w_up: bfloat16 [2, 1024, 2048], P('section'), may hold values from -0.1875 to 0.1875
- w_down: bfloat16 [2, 2048, 1024], P('section'), may hold values from -0.1875 to 0.1875
- gains: float32 [2, 2, 1024], P('section'), may hold values from 0.5 to 1.5
- biases: float32 [2, 2, 1024], P('section'), may hold values from -3 to 3
Outputs:
- layer_outputs: bfloat16 [2, 4096, 1024], P('section', ('dp', 'rep'))
- input_grads: bfloat16 [2, 4096, 1024], P('section', ('dp', 'rep'))
- grad_qkv: float32 [2, 1024, 3072], P('section', 'dp')
- grad_wout: float32 [2, 1024, 1024], P('section', None, 'dp')
- grad_up: float32 [2, 1024, 2048], P('section', 'dp')
- grad_down: float32 [2, 2048, 1024], P('section', None, 'dp')
- grad_gains: float32 [2, 2, 1024], P('section', None, 'dp')
- grad_biases: float32 [2, 2, 1024], P('section', None, 'dp')
Inputs may be any that keep to these rules, and one draw needn't show every extreme that they name: seg_counts gives each series' number of valid slots; the first 16 - seg_counts slots of a series are padding.
All inputs are finite; a program needn't handle non-finite values.
Results may differ from a plain program's by a relative error of at most 0.015.
Values may be sent and summed in bfloat16 or wider, within the bound.
A program may use at most 256 MiB of HBM per device.

v0:
```python
from functools import partial
import jax
import jax.numpy as jnp
from jax import lax
from jax.sharding import PartitionSpec as P

SEG = 16
MB_SER = 8
HEAD_DIM = 128
epsilon = 1e-05


def from_behind(block, axis, distance):
    devices = range(lax.axis_size(axis))
    route = [(i - distance, i) for i in devices if i - distance in devices]
    return lax.ppermute(block, axis, route)


def normalize(hidden):
    average = jnp.mean(hidden, axis=-1, keepdims=True)
    centred = hidden - average
    inverse = lax.rsqrt(jnp.mean(centred * centred, axis=-1, keepdims=True) + epsilon)
    return (centred * inverse, inverse)


def normalize_back(grad_normed, normed, inverse):
    centre_term = jnp.mean(grad_normed, axis=-1, keepdims=True)
    slope_term = normed * jnp.mean(grad_normed * normed, axis=-1, keepdims=True)
    return inverse * (grad_normed - centre_term - slope_term)


def allowed_pairs(counts):
    number = counts.shape[0]
    rows = number * SEG
    position = jnp.broadcast_to(jnp.arange(SEG, dtype=jnp.int32)[None, :], (number, SEG)).reshape(
        rows
    )
    first = jnp.broadcast_to((SEG - counts)[:, None], (number, SEG)).reshape(rows)
    owner = jnp.broadcast_to(jnp.arange(number, dtype=jnp.int32)[:, None], (number, SEG)).reshape(
        rows
    )
    row_ids = jnp.arange(rows, dtype=jnp.int32)
    same_series = owner[:, None] == owner[None, :]
    causal = position[None, :] <= position[:, None]
    valid = (position >= first)[None, :] | (row_ids[:, None] == row_ids[None, :])
    return same_series & causal & valid


def probabilities(queries, keys_in, allowed):
    scores = jnp.einsum(
        "qhd,khd->hqk", queries, keys_in, preferred_element_type=jnp.float32
    ) * HEAD_DIM ** (-0.5)
    scores = jnp.where(allowed[None], scores, -1e30)
    largest = jnp.max(scores, axis=-1, keepdims=True)
    raised = jnp.exp(scores - largest)
    return raised / jnp.sum(raised, axis=-1, keepdims=True)


def keep_local(value):
    return value


def layer_forward(hidden_b, params, allowed, joins):
    w_qkv, w_out, w_up, w_down, gains, biases = params
    attention_join, feed_join = (joins[0], joins[1])
    rows = hidden_b.shape[0]
    local_heads = w_qkv.shape[1] // (3 * HEAD_DIM)
    hidden = hidden_b.astype(jnp.float32)
    normed_one, inverse_one = normalize(hidden)
    first_b = (normed_one * gains[0] + biases[0]).astype(jnp.bfloat16)
    packed_b = jnp.dot(first_b, w_qkv, preferred_element_type=jnp.float32).astype(jnp.bfloat16)
    split = packed_b.reshape(rows, 3, local_heads, HEAD_DIM)
    probs = probabilities(split[:, 0], split[:, 1], allowed)
    probs_b = probs.astype(jnp.bfloat16)
    mixed = jnp.einsum("hqk,khd->qhd", probs_b, split[:, 2], preferred_element_type=jnp.float32)
    mixed_b = mixed.reshape(rows, local_heads * HEAD_DIM).astype(jnp.bfloat16)
    middle = hidden + attention_join(jnp.dot(mixed_b, w_out, preferred_element_type=jnp.float32))
    normed_two, inverse_two = normalize(middle)
    second_b = (normed_two * gains[1] + biases[1]).astype(jnp.bfloat16)
    upper = jnp.dot(second_b, w_up, preferred_element_type=jnp.float32)
    active_b = jax.nn.gelu(upper, approximate=True).astype(jnp.bfloat16)
    result_b = (
        middle + feed_join(jnp.dot(active_b, w_down, preferred_element_type=jnp.float32))
    ).astype(jnp.bfloat16)
    saved = (
        normed_one,
        inverse_one,
        first_b,
        split,
        probs,
        probs_b,
        mixed_b,
        normed_two,
        inverse_two,
        second_b,
        upper,
        active_b,
    )
    return (result_b, saved)


def layer_backward(hidden_b, grad_b, params, allowed, joins):
    w_qkv, w_out, w_up, w_down, gains, biases = params
    feed_back, attention_back = (joins[2], joins[3])
    rows = hidden_b.shape[0]
    local_heads = w_qkv.shape[1] // (3 * HEAD_DIM)
    saved = layer_forward(hidden_b, params, allowed, joins)[1]
    (
        normed_one,
        inverse_one,
        first_b,
        split,
        probs,
        probs_b,
        mixed_b,
        normed_two,
        inverse_two,
        second_b,
        upper,
        active_b,
    ) = saved
    grad_result = grad_b.astype(jnp.float32)
    grad_down = jnp.einsum("rf,rd->fd", active_b, grad_b, preferred_element_type=jnp.float32)
    grad_active = jnp.einsum("rd,fd->rf", grad_b, w_down, preferred_element_type=jnp.float32)
    grad_upper = jax.vjp(partial(jax.nn.gelu, approximate=True), upper)[1](grad_active)[0]
    grad_upper_b = grad_upper.astype(jnp.bfloat16)
    grad_up = jnp.einsum("rd,rf->df", second_b, grad_upper_b, preferred_element_type=jnp.float32)
    grad_second = feed_back(
        jnp.einsum("rf,df->rd", grad_upper_b, w_up, preferred_element_type=jnp.float32)
    )
    grad_middle = grad_result + normalize_back(grad_second * gains[1], normed_two, inverse_two)
    grad_middle_b = grad_middle.astype(jnp.bfloat16)
    grad_wout = jnp.einsum("ri,ro->io", mixed_b, grad_middle_b, preferred_element_type=jnp.float32)
    grad_mixed = jnp.einsum("ro,io->ri", grad_middle_b, w_out, preferred_element_type=jnp.float32)
    grad_mixed_b = grad_mixed.astype(jnp.bfloat16).reshape(rows, local_heads, HEAD_DIM)
    grad_probs = jnp.einsum(
        "qhd,khd->hqk", grad_mixed_b, split[:, 2], preferred_element_type=jnp.float32
    )
    grad_values = jnp.einsum(
        "hqk,qhd->khd", probs_b, grad_mixed_b, preferred_element_type=jnp.float32
    )
    grad_scores = probs * (grad_probs - jnp.sum(probs * grad_probs, axis=-1, keepdims=True))
    grad_scores_b = grad_scores.astype(jnp.bfloat16)
    grad_queries = jnp.einsum(
        "hqk,khd->qhd", grad_scores_b, split[:, 1], preferred_element_type=jnp.float32
    ) * HEAD_DIM ** (-0.5)
    grad_keys = jnp.einsum(
        "hqk,qhd->khd", grad_scores_b, split[:, 0], preferred_element_type=jnp.float32
    ) * HEAD_DIM ** (-0.5)
    grad_packed = jnp.stack((grad_queries, grad_keys, grad_values), axis=1)
    grad_packed_b = grad_packed.reshape(rows, 3 * local_heads * HEAD_DIM).astype(jnp.bfloat16)
    grad_qkv = jnp.einsum("rd,re->de", first_b, grad_packed_b, preferred_element_type=jnp.float32)
    grad_first = attention_back(
        jnp.einsum("re,de->rd", grad_packed_b, w_qkv, preferred_element_type=jnp.float32)
    )
    grad_hidden = grad_middle + normalize_back(grad_first * gains[0], normed_one, inverse_one)
    grad_gains = jnp.stack(
        (jnp.sum(grad_first * normed_one, axis=0), jnp.sum(grad_second * normed_two, axis=0))
    )
    grad_biases = jnp.stack((jnp.sum(grad_first, axis=0), jnp.sum(grad_second, axis=0)))
    return (grad_hidden, (grad_qkv, grad_wout, grad_up, grad_down, grad_gains, grad_biases))


def per_device(inputs, cotangent, seg_counts, w_qkv, w_out, w_up, w_down, gains, biases):
    sections = lax.axis_size("section")
    section = lax.axis_index("section")
    rows = MB_SER * SEG
    width = inputs.shape[1]
    micro = inputs.shape[0] // rows
    ticks = micro + sections - 1
    pairs = 1
    feed_rows = inputs.reshape(micro, rows, width)
    back_rows = cotangent.reshape(micro, rows, width)
    count_rows = seg_counts.reshape(micro, MB_SER)
    params = (w_qkv[0], w_out[0], w_up[0], w_down[0], gains[0], biases[0])
    joins = (keep_local, keep_local, keep_local, keep_local)
    block_rows = pairs * rows
    zero_terms = tuple((jnp.zeros(weight.shape, jnp.float32) for weight in params))

    def forward_tick(tick, carry):
        arrived, kept, results = carry
        position = tick - section
        active = (position >= 0) & (position < micro)
        slot = jnp.clip(position, 0, micro - 1)
        source = jnp.where(section == 0, feed_rows[slot], arrived)
        allowed = allowed_pairs(count_rows[slot])
        result = lax.cond(
            active,
            lambda state: layer_forward(state, params, allowed, joins)[0],
            lambda state: jnp.zeros_like(state),
            source,
        )
        kept = jnp.where(active, lax.dynamic_update_slice_in_dim(kept, source[None], slot, 0), kept)
        results = jnp.where(
            active, lax.dynamic_update_slice_in_dim(results, result[None], slot, 0), results
        )
        arrived = from_behind(result, "section", 1)
        return (arrived, kept, results)

    empty_rows = jnp.zeros((block_rows, width), jnp.bfloat16)
    empty_store = jnp.zeros((micro, block_rows, width), jnp.bfloat16)
    _, kept, results = lax.fori_loop(0, ticks, forward_tick, (empty_rows, empty_store, empty_store))

    def backward_tick(tick, carry):
        arrived, totals, returned = carry
        position = tick - (sections - 1 - section)
        active = (position >= 0) & (position < micro)
        slot = jnp.clip(position, 0, micro - 1)
        upstream = jnp.where(section == sections - 1, back_rows[slot], arrived)
        allowed = allowed_pairs(count_rows[slot])
        layer_input = kept[slot]

        def run_layer(state):
            grad_hidden, terms = layer_backward(layer_input, state, params, allowed, joins)
            return (grad_hidden.astype(jnp.bfloat16), terms)

        def skip_layer(state):
            return (jnp.zeros_like(state), zero_terms)

        grad_hidden_b, terms = lax.cond(active, run_layer, skip_layer, upstream)
        totals = tuple((total + term for total, term in zip(totals, terms)))
        returned = jnp.where(
            active,
            lax.dynamic_update_slice_in_dim(returned, grad_hidden_b[None], slot, 0),
            returned,
        )
        arrived = from_behind(grad_hidden_b, "section", -1)
        return (arrived, totals, returned)

    _, totals, returned = lax.fori_loop(
        0, ticks, backward_tick, (empty_rows, zero_terms, empty_store)
    )
    shares = (
        lax.psum_scatter(totals[0][None], "dp", scatter_dimension=1, tiled=True),
        lax.psum_scatter(totals[1][None], "dp", scatter_dimension=2, tiled=True),
        lax.psum_scatter(totals[2][None], "dp", scatter_dimension=1, tiled=True),
        lax.psum_scatter(totals[3][None], "dp", scatter_dimension=2, tiled=True),
        lax.psum_scatter(totals[4][None], "dp", scatter_dimension=2, tiled=True),
        lax.psum_scatter(totals[5][None], "dp", scatter_dimension=2, tiled=True),
    )
    summed = (
        lax.psum(shares[0].astype(jnp.bfloat16), "rep").astype(jnp.float32),
        lax.psum(shares[1].astype(jnp.bfloat16), "rep").astype(jnp.float32),
        lax.psum(shares[2].astype(jnp.bfloat16), "rep").astype(jnp.float32),
        lax.psum(shares[3].astype(jnp.bfloat16), "rep").astype(jnp.float32),
        lax.psum(shares[4].astype(jnp.bfloat16), "rep").astype(jnp.float32),
        lax.psum(shares[5].astype(jnp.bfloat16), "rep").astype(jnp.float32),
    )
    layer_outputs = results.reshape(1, micro * rows, width)
    input_grads = returned.reshape(1, micro * rows, width)
    return (
        layer_outputs,
        input_grads,
        summed[0],
        summed[1],
        summed[2],
        summed[3],
        summed[4],
        summed[5],
    )


def solution(mesh):
    placed = (
        P(("dp", "rep"), None),
        P(("dp", "rep"), None),
        P(("dp", "rep")),
        P("section", None, None),
        P("section", None, None),
        P("section", None, None),
        P("section", None, None),
        P("section", None, None),
        P("section", None, None),
    )
    return jax.shard_map(
        per_device,
        mesh=mesh,
        in_specs=placed,
        out_specs=(
            P("section", ("dp", "rep"), None),
            P("section", ("dp", "rep"), None),
            P("section", "dp", None),
            P("section", None, "dp"),
            P("section", "dp", None),
            P("section", None, "dp"),
            P("section", None, "dp"),
            P("section", None, "dp"),
        ),
        check_vma=False,
    )
```

profile of v0, /device:TPU:0, one launch (start us, length us, event | category | flops | bytes accessed | tf_op | source)
XLA Modules:
  0.0 1205.0 jit_solution(18255057795434790949)
XLA Ops:
  9.5 80.4 %while.48 = (s32[]{:T(128)}, bf16[128,1024]{1,0:T(8,128)(2,1)S(1)}, bf16[2,128,1024]{2,1,0:T(8,128)(2,1)S(1)}, bf16[2,128,1024]{2,1,0:T(8,128)(2,1)}, s32[]{:T(1...) while((s32[]{:T(128)}, bf16[128,1024]{1,0:T(8,128)(2,1)S(1)}, ...), condition=%wide.region_9.10_spmd, body=%wide.region_0.9_spmd.sunk | while | flops 2222163456 | bytes 41540956 | solution.py:202
  10.7 22.2 %conditional.5 = (bf16[128,1024]{1,0:T(8,128)(2,1)}, bf16[1,128,1024]{2,1,0:T(8,128)(2,1)}) conditional(s32[]{:T(128)} %convert_element_type.348, () %tuple.146, (bf16[128,1024]{1,0:T(8,128)(2,1)S(1)}, f32[2,1024]{1,0:T(2,128)}, f32[2,1024]{1,0:T(2,128)}, bf16[1024,3072]{1,0:T(8,128)(2,1)}, s32[8,16]{1,0:T(8,128)S(1)}, ...), branch_computations={%region_1.1_spmd, %region_2.8_spmd} | conditional | flops 2221770240 | bytes 38262244 | solution.py:187
  12.5 3.9 fusion.1
  25.4 5.8 fusion.5
  37.2 22.2 %conditional.5 = (bf16[128,1024]{1,0:T(8,128)(2,1)}, bf16[1,128,1024]{2,1,0:T(8,128)(2,1)}) conditional(s32[]{:T(128)} %convert_element_type.348, () %tuple.146, (bf16[128,1024]{1,0:T(8,128)(2,1)S(1)}, f32[2,1024]{1,0:T(2,128)}, f32[2,1024]{1,0:T(2,128)}, bf16[1024,3072]{1,0:T(8,128)(2,1)}, s32[8,16]{1,0:T(8,128)S(1)}, ...), branch_computations={%region_1.1_spmd, %region_2.8_spmd} | conditional | flops 2221770240 | bytes 38262244 | solution.py:187
  39.0 3.9 fusion.1
  51.9 5.8 fusion.5
  65.7 22.5 %collective-permute-start = (bf16[128,1024]{1,0:T(8,128)(2,1)}, bf16[128,1024]{1,0:T(8,128)(2,1)S(1)}, u32[]{:S(2)}, u32[]{:S(2)}) collective-permute-start(bf16[128,1024]{1,0:T(8,128)(2,1)} %get-tuple-element.1496), channel_id=1, source_target_pairs={{0,16},{1,17},{2,18},{3,19},{4,20},{5,21},{6,22},{7,23},{8,24},{9,... | collective-permute-start | bytes 786440 | tf_op jit(solution)/shard_map/while/body/eval_jaxpr/ppermute | solution.py:16
  91.5 296.8 %while.49 = (s32[]{:T(128)}, bf16[128,1024]{1,0:T(8,128)(2,1)}, f32[1024,3072]{1,0:T(8,128)}, f32[1024,1024]{1,0:T(8,128)}, f32[1024,2048]{1,0:T(8,128)}, /*inde...) while((s32[]{:T(128)}, bf16[128,1024]{1,0:T(8,128)(2,1)}, ...), condition=%wide.region_28.29_spmd.clone, body=%wide.region_10.28_spmd.clone.sunk | while | flops 6145549824 | bytes 265440848 | solution.py:230
  92.1 19.7 %conditional.6 = (bf16[128,1024]{1,0:T(8,128)(2,1)}, f32[1024,3072]{1,0:T(8,128)}, f32[1024,1024]{1,0:T(8,128)}, f32[1024,2048]{1,0:T(8,128)}, f32[2048,1024]{1,...) conditional(s32[]{:T(128)} %convert_element_type.349, () %tuple.150, ...), branch_computations={%region_11.11_spmd, %region_12.27_spmd} | conditional | flops 6128633344 | bytes 157386656 | solution.py:220
  92.1 6.1 broadcast_in_dim.241
  98.2 4.2 broadcast_in_dim.243
  102.4 4.3 broadcast_in_dim.244
  113.1 12.1 %select_add_fusion.11 = f32[1024,3072]{1,0:T(8,128)} fusion(f32[1024,3072]{1,0:T(8,128)} %get-tuple-element.1520, f32[1024,3072]{1,0:T(8,128)} %get-tuple-element.1625, pred[]{:T(512)S(6)} %compare.3), kind=kLoop, calls=%fused_computation.175.clone.1 | loop fusion | flops 6291456 | bytes 37748736 | tf_op jit(solution)/shard_map/while/body/eval_jaxpr/add | solution.py:221
  125.2 9.4 select_add_fusion.13
  134.6 9.6 select_add_fusion.14
  144.2 5.6 select_add_fusion.12
  150.7 8.0 collective-permute-done.1
  160.0 64.2 %conditional.6 = (bf16[128,1024]{1,0:T(8,128)(2,1)}, f32[1024,3072]{1,0:T(8,128)}, f32[1024,1024]{1,0:T(8,128)}, f32[1024,2048]{1,0:T(8,128)}, f32[2048,1024]{1,...) conditional(s32[]{:T(128)} %convert_element_type.349, () %tuple.150, ...), branch_computations={%region_11.11_spmd, %region_12.27_spmd} | conditional | flops 6128633344 | bytes 157386656 | solution.py:220
  161.2 3.9 fusion.48
  177.7 3.7 fusion.128
  183.9 4.6 fusion.116
  203.1 7.7 fusion.87
  214.4 2.6 fusion.101
  217.1 4.5 fusion.81
  225.5 14.9 %select_add_fusion.11 = f32[1024,3072]{1,0:T(8,128)} fusion(f32[1024,3072]{1,0:T(8,128)} %get-tuple-element.1520, f32[1024,3072]{1,0:T(8,128)} %get-tuple-element.1625, pred[]{:T(512)S(6)} %compare.3), kind=kLoop, calls=%fused_computation.175.clone.1 | loop fusion | flops 6291456 | bytes 37748736 | tf_op jit(solution)/shard_map/while/body/eval_jaxpr/add | solution.py:221
  240.5 11.8 select_add_fusion.13
  252.3 12.0 select_add_fusion.14
  264.3 6.9 select_add_fusion.12
  274.4 64.2 %conditional.6 = (bf16[128,1024]{1,0:T(8,128)(2,1)}, f32[1024,3072]{1,0:T(8,128)}, f32[1024,1024]{1,0:T(8,128)}, f32[1024,2048]{1,0:T(8,128)}, f32[2048,1024]{1,...) conditional(s32[]{:T(128)} %convert_element_type.349, () %tuple.150, ...), branch_computations={%region_11.11_spmd, %region_12.27_spmd} | conditional | flops 6128633344 | bytes 157386656 | solution.py:220
  275.6 3.9 fusion.48
  292.2 3.7 fusion.128
  298.3 4.6 fusion.116
  317.5 7.7 fusion.87
  328.9 2.6 fusion.101
  331.5 4.5 fusion.81
  340.0 14.9 %select_add_fusion.11 = f32[1024,3072]{1,0:T(8,128)} fusion(f32[1024,3072]{1,0:T(8,128)} %get-tuple-element.1520, f32[1024,3072]{1,0:T(8,128)} %get-tuple-element.1625, pred[]{:T(512)S(6)} %compare.3), kind=kLoop, calls=%fused_computation.175.clone.1 | loop fusion | flops 6291456 | bytes 37748736 | tf_op jit(solution)/shard_map/while/body/eval_jaxpr/add | solution.py:221
  354.9 11.8 select_add_fusion.13
  366.7 12.0 select_add_fusion.14
  378.7 6.9 select_add_fusion.12
  392.7 86.8 %reduce-scatter.13.cloned.1.call-done = f32[1,1024,128]{2,1,0:T(8,128)} async-done(((f32[1,1024,1024]{2,1,0:T(8,128)}), f32[1,1024,128]{2,1,0:T(8,128)}) %reduce-scatter.13.cloned.1.call-update) | async-done | bytes 524304 | tf_op jit(solution)/shard_map/reduce_scatter | solution.py:235
  481.4 151.1 %reduce-scatter.15.cloned.1.call-done = f32[1,128,2048]{2,1,0:T(8,128)} async-done(((f32[1,1024,2048]{2,1,0:T(8,128)}), f32[1,128,2048]{2,1,0:T(8,128)}) %reduce-scatter.15.cloned.1.call-update) | async-done | bytes 1048592 | tf_op jit(solution)/shard_map/reduce_scatter | solution.py:236
  634.5 150.0 %reduce-scatter.17.cloned.1.call-done = f32[1,2048,128]{2,1,0:T(8,128)} async-done(((f32[1,2048,1024]{2,1,0:T(8,128)}), f32[1,2048,128]{2,1,0:T(8,128)}) %reduce-scatter.17.cloned.1.call-update) | async-done | bytes 1048592 | tf_op jit(solution)/shard_map/reduce_scatter | solution.py:237
  786.6 208.1 %reduce-scatter.11.cloned.1.call-done = f32[1,128,3072]{2,1,0:T(8,128)} async-done(((f32[1,1024,3072]{2,1,0:T(8,128)}), f32[1,128,3072]{2,1,0:T(8,128)}) %reduce-scatter.11.cloned.1.call-update) | async-done | bytes 1572880 | tf_op jit(solution)/shard_map/reduce_scatter | solution.py:234
  997.1 62.8 %reduce-scatter.19.cloned.1.call-done = f32[128,2]{1,0:T(8,128)} async-done(((f32[1024,2]{1,0:T(8,128)}), f32[128,2]{1,0:T(8,128)}) %reduce-scatter.19.cloned.1.call-update) | async-done | bytes 1040
  1060.9 63.2 %reduce-scatter.21.cloned.1.call-done = f32[128,2]{1,0:T(8,128)} async-done(((f32[1024,2]{1,0:T(8,128)}), f32[128,2]{1,0:T(8,128)}) %reduce-scatter.21.cloned.1.call-update) | async-done | bytes 1040
  1125.0 4.9 all-reduce
  1131.1 58.7 %all-reduce.4.cloned.1.call-done = (bf16[1,128,3072]{2,1,0:T(8,128)(2,1)}, bf16[1,1024,128]{2,1,0:T(8,128)(2,1)}, bf16[1,128,2048]{2,1,0:T(8,128)(2,1)}, bf16[1,2048,128]{2,1,0:T(8,128)(2,1)}) async-done(((bf16[1,128,3072]{2,1,0:T(8,128)(2,1)}, bf16[1,1024,128]{2,1,0:T(8,128)(2,1)}, bf16[1,128,2048]{2,1,0:T(8,128)(2,1)}, bf16[1,2048,128]{2,1,0:T(8,128)(2,1)}), (bf16[1,128,3072]{2,1,0:T(8,128)(2,1)}, ...) | async-done | bytes 2097168 | tf_op jit(solution)/shard_map/psum | solution.py:242
  (356 shorter events, 158.7 us)
Async XLA Ops:
  7.2 472.4 %reduce-scatter.13.cloned.1.call-start = ((), (), s32[]{:S(2)}) async-start(), calls=%async_computation.7 | async-start | bytes 4718592 | tf_op jit(solution)/shard_map/reduce_scatter | solution.py:235
  16.4 7.3 copy-start
  18.3 7.2 copy-start.25
  32.9 3.1 collective-permute-start
  42.9 7.3 copy-start
  44.7 7.2 copy-start.25
  59.4 3.6 collective-permute-start
  65.7 24.3 %collective-permute-start = (bf16[128,1024]{1,0:T(8,128)(2,1)}, bf16[128,1024]{1,0:T(8,128)(2,1)S(1)}, u32[]{:S(2)}, u32[]{:S(2)}) collective-permute-start(bf16[128,1024]{1,0:T(8,128)(2,1)} %get-tuple-element.1496), channel_id=1, source_target_pairs={{0,16},{1,17},{2,18},{3,19},{4,20},{5,21},{6,22},{7,23},{8,24},{9,... | collective-permute-start | bytes 786440 | tf_op jit(solution)/shard_map/while/body/eval_jaxpr/ppermute | solution.py:16
  111.8 46.9 %collective-permute-start.1 = (bf16[128,1024]{1,0:T(8,128)(2,1)}, bf16[128,1024]{1,0:T(8,128)(2,1)S(1)}, u32[]{:S(2)}, u32[]{:S(2)}) collective-permute-start(bf16[128,1024]{1,0:T(8,128)(2,1)} %get-tuple-element.1519), channel_id=1, source_target_pairs={{16,0},{17,1},{18,2},{19,3},{20,4},{21,5},{22,6},{23,7},{24,8},{25... | collective-permute-start | bytes 786440 | tf_op jit(solution)/shard_map/while/body/eval_jaxpr/ppermute | solution.py:16
  144.2 6.4 copy-start.12
  150.6 8.2 copy-start.20
  150.6 8.2 copy-start.23
  150.7 8.1 copy-start.13
  165.1 10.3 copy-start.1
  165.5 7.4 copy-start.7
  165.5 16.0 %copy-start.8 = (bf16[128,1,8,128]{3,2,1,0:T(8,128)(2,1)}, bf16[128,1,8,128]{3,2,1,0:T(8,128)(2,1)S(1)}, u32[]{:S(2)}) copy-start(bf16[128,1,8,128]{3,2,1,0:T(8,128)(2,1)S(1)} %get-tuple-element.1274) | copy-start | bytes 786436 | tf_op jit(solution)/shard_map/while/body/eval_jaxpr/cond
  175.4 6.1 copy-start.5
  192.0 11.1 copy-start.16
  192.0 11.1 copy-start.18
  200.6 10.2 slice-start
  203.1 7.7 slice-start.1
  203.1 7.7 copy-start.2
  210.8 6.2 copy-start.4
  224.2 48.7 %collective-permute-start.1 = (bf16[128,1024]{1,0:T(8,128)(2,1)}, bf16[128,1024]{1,0:T(8,128)(2,1)S(1)}, u32[]{:S(2)}, u32[]{:S(2)}) collective-permute-start(bf16[128,1024]{1,0:T(8,128)(2,1)} %get-tuple-element.1519), channel_id=1, source_target_pairs={{16,0},{17,1},{18,2},{19,3},{20,4},{21,5},{22,6},{23,7},{24,8},{25... | collective-permute-start | bytes 786440 | tf_op jit(solution)/shard_map/while/body/eval_jaxpr/ppermute | solution.py:16
  264.3 6.9 copy-start.19
  264.3 6.9 copy-start.22
  264.3 7.6 copy-start.12
  279.5 10.3 copy-start.1
  279.9 7.4 copy-start.7
  279.9 16.0 %copy-start.8 = (bf16[128,1,8,128]{3,2,1,0:T(8,128)(2,1)}, bf16[128,1,8,128]{3,2,1,0:T(8,128)(2,1)S(1)}, u32[]{:S(2)}) copy-start(bf16[128,1,8,128]{3,2,1,0:T(8,128)(2,1)S(1)} %get-tuple-element.1274) | copy-start | bytes 786436 | tf_op jit(solution)/shard_map/while/body/eval_jaxpr/cond
  289.8 6.1 copy-start.5
  289.8 6.1 copy-start.3
  306.4 11.1 copy-start.16
  306.4 11.1 copy-start.18
  315.0 10.2 slice-start
  317.5 7.7 slice-start.1
  317.5 7.7 copy-start.2
  325.3 6.2 copy-start.4
  338.7 48.7 %collective-permute-start.1 = (bf16[128,1024]{1,0:T(8,128)(2,1)}, bf16[128,1024]{1,0:T(8,128)(2,1)S(1)}, u32[]{:S(2)}, u32[]{:S(2)}) collective-permute-start(bf16[128,1024]{1,0:T(8,128)(2,1)} %get-tuple-element.1519), channel_id=1, source_target_pairs={{16,0},{17,1},{18,2},{19,3},{20,4},{21,5},{22,6},{23,7},{24,8},{25... | collective-permute-start | bytes 786440 | tf_op jit(solution)/shard_map/while/body/eval_jaxpr/ppermute | solution.py:16
  378.7 6.9 copy-start.19
  378.7 6.9 copy-start.22
  378.7 7.6 copy-start.12
  388.3 244.2 %reduce-scatter.15.cloned.1.call-start = ((), (), s32[]{:S(2)}) async-start(), calls=%async_computation.8 | async-start | bytes 9437184 | tf_op jit(solution)/shard_map/reduce_scatter | solution.py:236
  389.0 395.5 %reduce-scatter.17.cloned.1.call-start = ((), (), s32[]{:S(2)}) async-start(), calls=%async_computation.9 | async-start | bytes 9437184 | tf_op jit(solution)/shard_map/reduce_scatter | solution.py:237
  389.8 605.0 %reduce-scatter.11.cloned.1.call-start = ((), (), s32[]{:S(2)}) async-start(), calls=%async_computation.6 | async-start | bytes 14155776 | tf_op jit(solution)/shard_map/reduce_scatter | solution.py:234
  390.3 669.6 %reduce-scatter.19.cloned.1.call-start = ((), (), s32[]{:S(2)}) async-start(), calls=%async_computation.10 | async-start | bytes 589824
  391.6 732.6 %reduce-scatter.21.cloned.1.call-start = ((), (), s32[]{:S(2)}) async-start(), calls=%async_computation.11 | async-start | bytes 589824
  392.7 797.1 %all-reduce.4.cloned.1.call-start = ((), (), s32[]{:S(2)}) async-start(), calls=%async_computation.12 | async-start | bytes 4194304 | tf_op jit(solution)/shard_map/psum | solution.py:242
  (30 other events, 88.1 us)
Sparse Core Ops, SparseCore 0:
  388.4 91.1 reduce-scatter.12
  483.6 148.7 reduce-scatter.14
  636.1 148.3 reduce-scatter.16
  788.4 206.2 reduce-scatter.10
  998.9 61.0 reduce-scatter.18
  1063.2 60.8 reduce-scatter.20
  1127.3 62.4 all-reduce.3
where the time goes:
time: 1210 us
  waiting for transfers between devices  791 us (65%)
  other arithmetic  180 us (15%)
  matrix products  115 us (10%)
  local copies, waits for them, and re-layouts  68.8 us (6%)
  starting transfers between devices  29.8 us (2%)
  between operations  14.2 us (1%)
    reduce_scatter x1, waiting for transfers between devices, per_device(): lax.psum_scatter(totals[0][None], 'dp', scatter_dimension=1, tiled=True)  208 us
    reduce_scatter x1, waiting for transfers between devices, per_device(): lax.psum_scatter(totals[2][None], 'dp', scatter_dimension=1, tiled=True)  151 us
    reduce_scatter x1, waiting for transfers between devices, per_device(): lax.psum_scatter(totals[3][None], 'dp', scatter_dimension=2, tiled=True)  150 us
    add x15, other arithmetic, backward_tick(): totals = tuple((total + term for total, term in zip(totals, terms)))  130 us
    unnamed x9, waiting for transfers between devices  128 us
    reduce_scatter x1, waiting for transfers between devices, per_device(): lax.psum_scatter(totals[1][None], 'dp', scatter_dimension=2, tiled=True)  86.8 us
    psum x1, waiting for transfers between devices, per_device(): lax.psum(shares[0].astype(jnp.bfloat16), 'rep').astype(jnp.float32)  58.7 us
    ppermute x6, starting transfers between devices, from_behind(): return lax.ppermute(block, axis, route)  29.5 us
  transfers between devices with their start and end apart: 13, of which 8 were waited for; matrix products, arithmetic and copies ran while one was open for 13% of the time, Pallas kernels for 0%

commit v1 on v0

--- a/solution.py
+++ b/solution.py
@@ -239,7 +239,7 @@
         lax.psum_scatter(totals[5][None], "dp", scatter_dimension=2, tiled=True),
     )
     summed = (
-        lax.psum(shares[0].astype(jnp.bfloat16), "rep").astype(jnp.float32),
+        jnp.sum(lax.all_gather(shares[0].astype(jnp.bfloat16), "rep"), axis=0).astype(jnp.float32),
         lax.psum(shares[1].astype(jnp.bfloat16), "rep").astype(jnp.float32),
         lax.psum(shares[2].astype(jnp.bfloat16), "rep").astype(jnp.float32),
         lax.psum(shares[3].astype(jnp.bfloat16), "rep").astype(jnp.float32),

time: 1210 us -> 1210 us (level)
    all_gather x0 -> x1, waiting for transfers between devices: none -> 23.4 us  [per_device(): lax.all_gather(shares[0].astype(jnp.bfloat16), 'rep')]
    psum x1, waiting for transfers between devices: 58.7 us -> 41.3 us  [per_device(): lax.psum(shares[1].astype(jnp.bfloat16), 'rep').astype(jnp.float32)]
    unnamed x9 -> x10, waiting for transfers between devices: 128 us -> 128 us
  transfers between devices with their start and end apart: 13 -> 14, of which waited for: 8 -> 9; matrix products, arithmetic and copies ran while one was open for 13% -> 13% of each run, Pallas kernels for 0% -> 0%
where the time goes in v1:
time: 1210 us
  waiting for transfers between devices  797 us (66%)
  other arithmetic  181 us (15%)
  matrix products  115 us (10%)
  local copies, waits for them, and re-layouts  68.8 us (6%)
  starting transfers between devices  29.8 us (2%)
  between operations  14.2 us (1%)
    reduce_scatter x1, waiting for transfers between devices, per_device(): lax.psum_scatter(totals[0][None], 'dp', scatter_dimension=1, tiled=True)  208 us
    reduce_scatter x1, waiting for transfers between devices, per_device(): lax.psum_scatter(totals[2][None], 'dp', scatter_dimension=1, tiled=True)  151 us
    reduce_scatter x1, waiting for transfers between devices, per_device(): lax.psum_scatter(totals[3][None], 'dp', scatter_dimension=2, tiled=True)  150 us
    add x15, other arithmetic, backward_tick(): totals = tuple((total + term for total, term in zip(totals, terms)))  130 us
    unnamed x10, waiting for transfers between devices  128 us
    reduce_scatter x1, waiting for transfers between devices, per_device(): lax.psum_scatter(totals[1][None], 'dp', scatter_dimension=2, tiled=True)  86.8 us
    psum x1, waiting for transfers between devices, per_device(): lax.psum(shares[1].astype(jnp.bfloat16), 'rep').astype(jnp.float32)  41.3 us
    ppermute x6, starting transfers between devices, from_behind(): return lax.ppermute(block, axis, route)  29.5 us
  transfers between devices with their start and end apart: 14, of which 9 were waited for; matrix products, arithmetic and copies ran while one was open for 13% of the time, Pallas kernels for 0%

profile of v1, /device:TPU:0, one launch (start us, length us, event | category | flops | bytes accessed | tf_op | source)
XLA Modules:
  0.0 1211.7 jit_solution(15860973991415784357)
XLA Ops:
  9.5 80.4 %while.48 = (s32[]{:T(128)}, bf16[128,1024]{1,0:T(8,128)(2,1)S(1)}, bf16[2,128,1024]{2,1,0:T(8,128)(2,1)S(1)}, bf16[2,128,1024]{2,1,0:T(8,128)(2,1)}, s32[]{:T(1...) while((s32[]{:T(128)}, bf16[128,1024]{1,0:T(8,128)(2,1)S(1)}, ...), condition=%wide.region_9.10_spmd, body=%wide.region_0.9_spmd.sunk | while | flops 2222163456 | bytes 41540956 | solution.py:202
  10.7 22.2 %conditional.5 = (bf16[128,1024]{1,0:T(8,128)(2,1)}, bf16[1,128,1024]{2,1,0:T(8,128)(2,1)}) conditional(s32[]{:T(128)} %convert_element_type.363, () %tuple.146, (bf16[128,1024]{1,0:T(8,128)(2,1)S(1)}, f32[2,1024]{1,0:T(2,128)}, f32[2,1024]{1,0:T(2,128)}, bf16[1024,3072]{1,0:T(8,128)(2,1)}, s32[8,16]{1,0:T(8,128)S(1)}, ...), branch_computations={%region_1.1_spmd, %region_2.8_spmd} | conditional | flops 2221770240 | bytes 38262244 | solution.py:187
  12.5 3.9 fusion.1
  25.4 5.8 fusion.5
  37.2 22.2 %conditional.5 = (bf16[128,1024]{1,0:T(8,128)(2,1)}, bf16[1,128,1024]{2,1,0:T(8,128)(2,1)}) conditional(s32[]{:T(128)} %convert_element_type.363, () %tuple.146, (bf16[128,1024]{1,0:T(8,128)(2,1)S(1)}, f32[2,1024]{1,0:T(2,128)}, f32[2,1024]{1,0:T(2,128)}, bf16[1024,3072]{1,0:T(8,128)(2,1)}, s32[8,16]{1,0:T(8,128)S(1)}, ...), branch_computations={%region_1.1_spmd, %region_2.8_spmd} | conditional | flops 2221770240 | bytes 38262244 | solution.py:187
  39.0 3.9 fusion.1
  51.9 5.8 fusion.5
  65.7 22.5 %collective-permute-start = (bf16[128,1024]{1,0:T(8,128)(2,1)}, bf16[128,1024]{1,0:T(8,128)(2,1)S(1)}, u32[]{:S(2)}, u32[]{:S(2)}) collective-permute-start(bf16[128,1024]{1,0:T(8,128)(2,1)} %get-tuple-element.1495), channel_id=1, source_target_pairs={{0,16},{1,17},{2,18},{3,19},{4,20},{5,21},{6,22},{7,23},{8,24},{9,... | collective-permute-start | bytes 786440 | tf_op jit(solution)/shard_map/while/body/eval_jaxpr/ppermute | solution.py:16
  91.5 296.8 %while.49 = (s32[]{:T(128)}, bf16[128,1024]{1,0:T(8,128)(2,1)}, f32[1024,3072]{1,0:T(8,128)}, f32[1024,1024]{1,0:T(8,128)}, f32[1024,2048]{1,0:T(8,128)}, /*inde...) while((s32[]{:T(128)}, bf16[128,1024]{1,0:T(8,128)(2,1)}, ...), condition=%wide.region_28.29_spmd.clone, body=%wide.region_10.28_spmd.clone.sunk | while | flops 6145549824 | bytes 265440848 | solution.py:230
  92.1 19.7 %conditional.6 = (bf16[128,1024]{1,0:T(8,128)(2,1)}, f32[1024,3072]{1,0:T(8,128)}, f32[1024,1024]{1,0:T(8,128)}, f32[1024,2048]{1,0:T(8,128)}, f32[2048,1024]{1,...) conditional(s32[]{:T(128)} %convert_element_type.364, () %tuple.150, ...), branch_computations={%region_11.11_spmd, %region_12.27_spmd} | conditional | flops 6128633344 | bytes 157386656 | solution.py:220
  92.1 6.1 broadcast_in_dim.241
  98.2 4.2 broadcast_in_dim.243
  102.4 4.3 broadcast_in_dim.244
  113.1 12.1 select_add_fusion.11
  125.2 9.4 select_add_fusion.13
  134.6 9.6 select_add_fusion.14
  144.2 5.6 select_add_fusion.12
  150.7 8.0 collective-permute-done.1
  160.0 64.2 %conditional.6 = (bf16[128,1024]{1,0:T(8,128)(2,1)}, f32[1024,3072]{1,0:T(8,128)}, f32[1024,1024]{1,0:T(8,128)}, f32[1024,2048]{1,0:T(8,128)}, f32[2048,1024]{1,...) conditional(s32[]{:T(128)} %convert_element_type.364, () %tuple.150, ...), branch_computations={%region_11.11_spmd, %region_12.27_spmd} | conditional | flops 6128633344 | bytes 157386656 | solution.py:220
  161.2 3.9 fusion.48
  177.7 3.7 fusion.128
  183.9 4.6 fusion.116
  203.1 7.7 fusion.87
  214.4 2.6 fusion.101
  217.1 4.5 fusion.81
  225.5 14.9 %select_add_fusion.11 = f32[1024,3072]{1,0:T(8,128)} fusion(f32[1024,3072]{1,0:T(8,128)} %get-tuple-element.1519, f32[1024,3072]{1,0:T(8,128)} %get-tuple-element.1624, pred[]{:T(512)S(6)} %compare.3), kind=kLoop, calls=%fused_computation.175.clone.1 | loop fusion | flops 6291456 | bytes 37748736 | tf_op jit(solution)/shard_map/while/body/eval_jaxpr/add | solution.py:221
  240.5 11.8 select_add_fusion.13
  252.3 12.0 select_add_fusion.14
  264.3 6.9 select_add_fusion.12
  274.4 64.2 %conditional.6 = (bf16[128,1024]{1,0:T(8,128)(2,1)}, f32[1024,3072]{1,0:T(8,128)}, f32[1024,1024]{1,0:T(8,128)}, f32[1024,2048]{1,0:T(8,128)}, f32[2048,1024]{1,...) conditional(s32[]{:T(128)} %convert_element_type.364, () %tuple.150, ...), branch_computations={%region_11.11_spmd, %region_12.27_spmd} | conditional | flops 6128633344 | bytes 157386656 | solution.py:220
  275.6 3.9 fusion.48
  292.2 3.7 fusion.128
  298.3 4.6 fusion.116
  317.5 7.7 fusion.87
  331.5 4.5 fusion.81
  340.0 14.9 %select_add_fusion.11 = f32[1024,3072]{1,0:T(8,128)} fusion(f32[1024,3072]{1,0:T(8,128)} %get-tuple-element.1519, f32[1024,3072]{1,0:T(8,128)} %get-tuple-element.1624, pred[]{:T(512)S(6)} %compare.3), kind=kLoop, calls=%fused_computation.175.clone.1 | loop fusion | flops 6291456 | bytes 37748736 | tf_op jit(solution)/shard_map/while/body/eval_jaxpr/add | solution.py:221
  354.9 11.8 select_add_fusion.13
  366.7 12.0 select_add_fusion.14
  378.7 6.9 select_add_fusion.12
  392.7 86.8 %reduce-scatter.13.cloned.1.call-done = f32[1,1024,128]{2,1,0:T(8,128)} async-done(((f32[1,1024,1024]{2,1,0:T(8,128)}), f32[1,1024,128]{2,1,0:T(8,128)}) %reduce-scatter.13.cloned.1.call-update) | async-done | bytes 524304 | tf_op jit(solution)/shard_map/reduce_scatter | solution.py:235
  481.4 151.1 %reduce-scatter.15.cloned.1.call-done = f32[1,128,2048]{2,1,0:T(8,128)} async-done(((f32[1,1024,2048]{2,1,0:T(8,128)}), f32[1,128,2048]{2,1,0:T(8,128)}) %reduce-scatter.15.cloned.1.call-update) | async-done | bytes 1048592 | tf_op jit(solution)/shard_map/reduce_scatter | solution.py:236
  634.5 150.0 %reduce-scatter.17.cloned.1.call-done = f32[1,2048,128]{2,1,0:T(8,128)} async-done(((f32[1,2048,1024]{2,1,0:T(8,128)}), f32[1,2048,128]{2,1,0:T(8,128)}) %reduce-scatter.17.cloned.1.call-update) | async-done | bytes 1048592 | tf_op jit(solution)/shard_map/reduce_scatter | solution.py:237
  786.7 208.0 %reduce-scatter.11.cloned.1.call-done = f32[1,128,3072]{2,1,0:T(8,128)} async-done(((f32[1,1024,3072]{2,1,0:T(8,128)}), f32[1,128,3072]{2,1,0:T(8,128)}) %reduce-scatter.11.cloned.1.call-update) | async-done | bytes 1572880 | tf_op jit(solution)/shard_map/reduce_scatter | solution.py:234
  997.1 62.8 %reduce-scatter.19.cloned.1.call-done = f32[128,2]{1,0:T(8,128)} async-done(((f32[1024,2]{1,0:T(8,128)}), f32[128,2]{1,0:T(8,128)}) %reduce-scatter.19.cloned.1.call-update) | async-done | bytes 1040
  1060.9 63.2 %reduce-scatter.21.cloned.1.call-done = f32[128,2]{1,0:T(8,128)} async-done(((f32[1024,2]{1,0:T(8,128)}), f32[128,2]{1,0:T(8,128)}) %reduce-scatter.21.cloned.1.call-update) | async-done | bytes 1040
  1125.0 4.9 all-reduce
  1131.1 41.3 %all-reduce.4.cloned.1.call-done = (bf16[1,1024,128]{2,1,0:T(8,128)(2,1)}, bf16[1,128,2048]{2,1,0:T(8,128)(2,1)}, bf16[1,2048,128]{2,1,0:T(8,128)(2,1)}) async-done(((bf16[1,1024,128]{2,1,0:T(8,128)(2,1)}, bf16[1,128,2048]{2,1,0:T(8,128)(2,1)}, bf16[1,2048,128]{2,1,0:T(8,128)(2,1)}), (bf16[1,1024,128]{2,1,0:T(8,128)(2,1)}, bf16[1,128,2048]{2,1,0:T(8,128)(2,1)}, ...) | async-done | bytes 1310736 | tf_op jit(solution)/shard_map/psum | solution.py:243
  1178.4 23.4 %all-gather.3.cloned.1.call-done = bf16[2,128,3072]{2,1,0:T(8,128)(2,1)} async-done(((bf16[1,128,3072]{2,1,0:T(8,128)(2,1)}), bf16[2,128,3072]{2,1,0:T(8,128)(2,1)}) %all-gather.3.cloned.1.call-update) | async-done | bytes 1572880 | tf_op jit(solution)/shard_map/all_gather | solution.py:242
  (360 shorter events, 162.1 us)
Async XLA Ops:
  7.2 472.4 %reduce-scatter.13.cloned.1.call-start = ((), (), s32[]{:S(2)}) async-start(), calls=%async_computation.7 | async-start | bytes 4718592 | tf_op jit(solution)/shard_map/reduce_scatter | solution.py:235
  16.4 7.3 copy-start
  18.3 7.2 copy-start.25
  32.9 3.1 collective-permute-start
  42.9 7.3 copy-start
  44.7 7.2 copy-start.25
  59.4 3.6 collective-permute-start
  65.7 24.3 %collective-permute-start = (bf16[128,1024]{1,0:T(8,128)(2,1)}, bf16[128,1024]{1,0:T(8,128)(2,1)S(1)}, u32[]{:S(2)}, u32[]{:S(2)}) collective-permute-start(bf16[128,1024]{1,0:T(8,128)(2,1)} %get-tuple-element.1495), channel_id=1, source_target_pairs={{0,16},{1,17},{2,18},{3,19},{4,20},{5,21},{6,22},{7,23},{8,24},{9,... | collective-permute-start | bytes 786440 | tf_op jit(solution)/shard_map/while/body/eval_jaxpr/ppermute | solution.py:16
  111.8 46.9 %collective-permute-start.1 = (bf16[128,1024]{1,0:T(8,128)(2,1)}, bf16[128,1024]{1,0:T(8,128)(2,1)S(1)}, u32[]{:S(2)}, u32[]{:S(2)}) collective-permute-start(bf16[128,1024]{1,0:T(8,128)(2,1)} %get-tuple-element.1518), channel_id=1, source_target_pairs={{16,0},{17,1},{18,2},{19,3},{20,4},{21,5},{22,6},{23,7},{24,8},{25... | collective-permute-start | bytes 786440 | tf_op jit(solution)/shard_map/while/body/eval_jaxpr/ppermute | solution.py:16
  144.2 6.4 copy-start.12
  150.6 8.2 copy-start.20
  150.6 8.2 copy-start.23
  150.7 8.1 copy-start.13
  165.1 10.3 copy-start.1
  165.5 7.4 copy-start.7
  165.5 16.0 %copy-start.8 = (bf16[128,1,8,128]{3,2,1,0:T(8,128)(2,1)}, bf16[128,1,8,128]{3,2,1,0:T(8,128)(2,1)S(1)}, u32[]{:S(2)}) copy-start(bf16[128,1,8,128]{3,2,1,0:T(8,128)(2,1)S(1)} %get-tuple-element.1273) | copy-start | bytes 786436 | tf_op jit(solution)/shard_map/while/body/eval_jaxpr/cond
  192.0 11.1 copy-start.16
  192.0 11.1 copy-start.18
  200.6 10.2 slice-start
  203.1 7.7 slice-start.1
  203.1 7.7 copy-start.2
  210.8 6.2 copy-start.4
  224.2 48.7 %collective-permute-start.1 = (bf16[128,1024]{1,0:T(8,128)(2,1)}, bf16[128,1024]{1,0:T(8,128)(2,1)S(1)}, u32[]{:S(2)}, u32[]{:S(2)}) collective-permute-start(bf16[128,1024]{1,0:T(8,128)(2,1)} %get-tuple-element.1518), channel_id=1, source_target_pairs={{16,0},{17,1},{18,2},{19,3},{20,4},{21,5},{22,6},{23,7},{24,8},{25... | collective-permute-start | bytes 786440 | tf_op jit(solution)/shard_map/while/body/eval_jaxpr/ppermute | solution.py:16
  264.3 6.9 copy-start.19
  264.3 6.9 copy-start.22
  264.3 7.6 copy-start.12
  279.5 10.3 copy-start.1
  279.9 7.4 copy-start.7
  279.9 16.0 %copy-start.8 = (bf16[128,1,8,128]{3,2,1,0:T(8,128)(2,1)}, bf16[128,1,8,128]{3,2,1,0:T(8,128)(2,1)S(1)}, u32[]{:S(2)}) copy-start(bf16[128,1,8,128]{3,2,1,0:T(8,128)(2,1)S(1)} %get-tuple-element.1273) | copy-start | bytes 786436 | tf_op jit(solution)/shard_map/while/body/eval_jaxpr/cond
  289.8 6.1 copy-start.5
  289.8 6.1 copy-start.3
  306.4 11.1 copy-start.16
  306.4 11.1 copy-start.18
  315.0 10.2 slice-start
  317.5 7.7 slice-start.1
  317.5 7.7 copy-start.2
  325.3 6.2 copy-start.4
  338.7 48.7 %collective-permute-start.1 = (bf16[128,1024]{1,0:T(8,128)(2,1)}, bf16[128,1024]{1,0:T(8,128)(2,1)S(1)}, u32[]{:S(2)}, u32[]{:S(2)}) collective-permute-start(bf16[128,1024]{1,0:T(8,128)(2,1)} %get-tuple-element.1518), channel_id=1, source_target_pairs={{16,0},{17,1},{18,2},{19,3},{20,4},{21,5},{22,6},{23,7},{24,8},{25... | collective-permute-start | bytes 786440 | tf_op jit(solution)/shard_map/while/body/eval_jaxpr/ppermute | solution.py:16
  378.7 6.9 copy-start.19
  378.7 6.9 copy-start.22
  378.7 7.6 copy-start.12
  388.3 244.2 %reduce-scatter.15.cloned.1.call-start = ((), (), s32[]{:S(2)}) async-start(), calls=%async_computation.8 | async-start | bytes 9437184 | tf_op jit(solution)/shard_map/reduce_scatter | solution.py:236
  389.0 395.5 %reduce-scatter.17.cloned.1.call-start = ((), (), s32[]{:S(2)}) async-start(), calls=%async_computation.9 | async-start | bytes 9437184 | tf_op jit(solution)/shard_map/reduce_scatter | solution.py:237
  389.8 605.0 %reduce-scatter.11.cloned.1.call-start = ((), (), s32[]{:S(2)}) async-start(), calls=%async_computation.6 | async-start | bytes 14155776 | tf_op jit(solution)/shard_map/reduce_scatter | solution.py:234
  390.3 669.6 %reduce-scatter.19.cloned.1.call-start = ((), (), s32[]{:S(2)}) async-start(), calls=%async_computation.11 | async-start | bytes 589824
  391.6 732.6 %reduce-scatter.21.cloned.1.call-start = ((), (), s32[]{:S(2)}) async-start(), calls=%async_computation.12 | async-start | bytes 589824
  392.7 779.7 %all-reduce.4.cloned.1.call-start = ((), (), s32[]{:S(2)}) async-start(), calls=%async_computation.13 | async-start | bytes 2621440 | tf_op jit(solution)/shard_map/psum | solution.py:243
  786.6 415.2 %all-gather.3.cloned.1.call-start = ((), (), s32[]{:S(2)}) async-start(), calls=%async_computation.10 | async-start | bytes 2359296 | tf_op jit(solution)/shard_map/all_gather | solution.py:242
  (31 other events, 94.2 us)
Sparse Core Ops, SparseCore 0:
  388.4 91.1 reduce-scatter.12
  483.6 148.7 reduce-scatter.14
  636.1 148.3 reduce-scatter.16
  788.4 206.2 reduce-scatter.10
  998.9 61.0 reduce-scatter.18
  1063.2 60.8 reduce-scatter.20
  1127.3 45.1 all-reduce.3
  1174.5 27.2 all-gather.2
